TPU v7x, 32 devices: a whole 2x2x4 slice. The times are simulated.
32 devices in a mesh: clip: 8 (over y, x, core), tm: 4 (over z).
Axes of the slice: x: 2, y: 2, z: 4, core: 2. Of those that a mesh axis runs over, the one named last changes fastest.
Arguments:
- latent: bfloat16 [8, 32, 8, 32, 16], P('clip', 'tm'), may hold values from -6 to 6
- offsets: int32 [8], P('clip'), may hold values from 0 to 16
- teacher: bfloat16 [8, 32, 8, 16, 384], P('clip', 'tm'), may hold values from -6 to 6
- w_in: bfloat16 [432, 384], replicated, may hold values from -0.3125 to 0.3125
- w_mid: bfloat16 [10368, 384], P('clip'), may hold values from -0.0625 to 0.0625
Outputs:
- grad_mid: float32 [10368, 384], P('clip')
- grad_in: float32 [432, 384], replicated
Inputs may be any that keep to these rules, and one draw needn't show every extreme that they name: `offsets`: each clip's crop start among the latent columns.
All inputs are finite; a program needn't handle non-finite values.
Results may differ from a plain program's by a relative error of at most 0.00095.
Values may be sent and summed in bfloat16 or wider, within the bound.
No kernel may reach another device: no remote copies, remote signals or barrier semaphores. Data moves between devices by JAX's collectives and lax.ppermute only.
A program may use at most 192 MiB of HBM per device.

v0:
```python
import math
import jax
import jax.numpy as jnp
from jax import lax
from jax.sharding import PartitionSpec as P


def passed_along(block, axis, distance):
    devices = range(lax.axis_size(axis))
    route = [(i - distance, i) for i in devices if i - distance in devices]
    return lax.ppermute(block, axis, route)


def tap_masks(count, rows, cols):
    place = jnp.arange(count, dtype=jnp.int32) % (rows * cols)
    row_pos = place // cols
    col_pos = place % cols
    masks = []
    for row_off in range(3):
        for col_off in range(3):
            good_row = (row_pos + row_off - 1 >= 0) & (row_pos + row_off - 1 < rows)
            good_col = (col_pos + col_off - 1 >= 0) & (col_pos + col_off - 1 < cols)
            masks.append((good_row & good_col).astype(jnp.bfloat16).reshape(count, 1))
    return masks


def tap_slices(extended, count, rows, cols, masks):
    margin = jnp.zeros((cols + 1, extended.shape[1]), extended.dtype)
    padded = jnp.concatenate([margin, extended, margin], axis=0)
    plane = rows * cols
    pieces = []
    for depth in range(3):
        for row_off in range(3):
            for col_off in range(3):
                first = depth * plane + row_off * cols + col_off
                pieces.append(padded[first : first + count] * masks[row_off * 3 + col_off])
    return pieces


def cross_dot(left, right):
    return lax.dot_general(
        left, right, (((0,), (0,)), ((), ())), preferred_element_type=jnp.float32
    )


def shards(latent, offsets, teacher, w_in, w_mid):
    frames = teacher.shape[1]
    rows = teacher.shape[2]
    cols = teacher.shape[3]
    chans = teacher.shape[4]
    plane = rows * cols
    count = frames * plane
    lat_chans = latent.shape[4]
    total_cells = lax.axis_size("clip") * lax.axis_size("tm") * count
    scale = 2.0 / math.sqrt(total_cells)
    masks = tap_masks(count, rows, cols)
    crop = lax.dynamic_slice_in_dim(latent[0], offsets[0], cols, axis=2).reshape(count, lat_chans)
    earlier = passed_along(crop[count - 2 * plane :], "tm", 1)
    crop_ext = jnp.concatenate([earlier, crop], axis=0)
    patch_in = jnp.concatenate(tap_slices(crop_ext, count, rows, cols, masks), axis=1)
    z_first = jnp.dot(patch_in, w_in, preferred_element_type=jnp.float32)
    act = jax.nn.silu(z_first).astype(jnp.bfloat16)
    act_prev = passed_along(act[count - 2 * plane :], "tm", 1)
    act_ext = jnp.concatenate([act_prev, act], axis=0)
    act_taps = tap_slices(act_ext, count, rows, cols, masks)
    w_full = lax.all_gather(w_mid, "clip", axis=0, tiled=True)
    output = jnp.zeros((count, chans), jnp.float32)
    for k in range(27):
        output = output + jnp.dot(
            act_taps[k], w_full[k * chans : (k + 1) * chans], preferred_element_type=jnp.float32
        )
    target_rows = teacher[0].reshape(count, chans).astype(jnp.float32)
    grad_low = ((output - target_rows) * scale).astype(jnp.bfloat16)
    local_mid = jnp.concatenate([cross_dot(act_taps[k], grad_low) for k in range(27)], axis=0)
    lead = 2 * plane + cols + 1
    masked_pads = []
    for k in range(9):
        masked_pads.append(jnp.pad(grad_low * masks[k], ((lead, lead), (0, 0))))
    ext_count = count + 2 * plane
    adjoint = jnp.zeros((ext_count, chans), jnp.float32)
    for depth in range(3):
        for row_off in range(3):
            for col_off in range(3):
                k = depth * 9 + row_off * 3 + col_off
                first = (2 - depth) * plane + (2 - row_off) * cols + (2 - col_off)
                piece = masked_pads[row_off * 3 + col_off][first : first + ext_count]
                adjoint = adjoint + lax.dot_general(
                    piece,
                    w_full[k * chans : (k + 1) * chans],
                    (((1,), (1,)), ((), ())),
                    preferred_element_type=jnp.float32,
                )
    outgoing = adjoint[: 2 * plane]
    incoming = passed_along(outgoing.astype(jnp.bfloat16), "tm", -1).astype(outgoing.dtype)
    own = adjoint[2 * plane :]
    dact = jnp.concatenate([own[: count - 2 * plane], own[count - 2 * plane :] + incoming], axis=0)
    sig = jax.nn.sigmoid(z_first)
    dz_first = (dact * sig * (1.0 + z_first * (1.0 - sig))).astype(jnp.bfloat16)
    grad_in = lax.psum(cross_dot(patch_in, dz_first), ("clip", "tm"))
    summed = lax.psum(local_mid, "tm")
    grad_mid = lax.psum_scatter(summed, "clip", scatter_dimension=0, tiled=True)
    return (grad_mid, grad_in)


def solution(mesh):
    return jax.shard_map(
        shards,
        mesh=mesh,
        in_specs=(
            P("clip", "tm", None, None, None),
            P("clip"),
            P("clip", "tm", None, None, None),
            P(),
            P("clip", None),
        ),
        out_specs=(P("clip", None), P()),
        check_vma=False,
    )
```

profile of v0, /device:TPU:0, one launch (start us, length us, event | category | flops | bytes accessed | tf_op | source)
XLA Modules:
  0.0 524.9 jit_solution(12850490637867089896)
XLA Ops:
  9.7 4.9 collective-permute-start
  18.5 2.0 multiply_convert_fusion
  20.5 3.9 collective-permute-start.1
  24.4 3.4 collective-permute-done.1
  27.8 2.3 concatenate.47
  30.2 35.1 %all-gather.2.cloned.1.call-done = bf16[10368,384]{1,0:T(8,128)(2,1)} async-done(((bf16[1296,384]{1,0:T(8,128)(2,1)}), bf16[10368,384]{1,0:T(8,128)(2,1)}) %all-gather.2.cloned.1.call-update) | async-done | bytes 7962640 | tf_op jit(solution)/shard_map/all_gather | solution.py:66
  65.3 3.0 fusion.52
  68.3 2.8 fusion.51
  71.1 2.8 fusion.50
  73.9 1.9 fusion.49
  75.8 1.9 fusion.132
  77.7 1.9 fusion.129
  79.5 1.9 fusion.126
  81.4 1.9 fusion.123
  83.3 1.8 fusion.120
  85.2 1.8 fusion.117
  87.0 1.9 fusion.114
  88.9 1.9 fusion.111
  90.7 1.9 fusion.108
  92.7 1.8 fusion.105
  94.5 1.9 fusion.102
  96.4 2.0 fusion.99
  98.4 1.9 fusion.96
  100.2 2.1 fusion.93
  102.3 1.9 fusion.90
  104.2 1.9 fusion.87
  106.1 1.9 fusion.84
  108.0 1.9 fusion.46
  109.9 1.9 fusion.47
  111.8 1.9 fusion.48
  113.7 1.9 fusion.45
  115.6 1.8 fusion.43
  117.4 17.8 %broadcast_multiply_fusion = (bf16[1024,384]{1,0:T(8,128)(2,1)S(1)}, bf16[1024,384]{1,0:T(8,128)(2,1)S(1)}, bf16[1024,384]{1,0:T(8,128)(2,1)S(1)}, bf16[1024,384...) fusion(bf16[1024]{0:T(1024)(128)(2,1)S(1)} %get-tuple-element.1, ...), kind=kOutput, calls=%fused_computation.165 | convolution fusion | flops 319684608 | bytes 50843648 | tf_op jit(solution)/shard_map/dot_general | solution.py:69
  135.3 3.1 convolution_dynamic-update-slice_fusion.26
  138.4 1.6 convolution_dynamic-update-slice_fusion.25
  144.9 1.6 convolution_dynamic-update-slice_fusion.21
  146.5 1.6 convolution_dynamic-update-slice_fusion.20
  148.2 1.6 convolution_dynamic-update-slice_fusion.19
  149.8 1.7 convolution_dynamic-update-slice_fusion.18
  151.5 1.6 convolution_dynamic-update-slice_fusion.17
  153.1 1.6 convolution_dynamic-update-slice_fusion.16
  154.7 1.6 convolution_dynamic-update-slice_fusion.15
  156.4 1.7 convolution_dynamic-update-slice_fusion.14
  158.0 1.7 convolution_dynamic-update-slice_fusion.13
  159.7 1.7 convolution_dynamic-update-slice_fusion.12
  161.4 1.6 convolution_dynamic-update-slice_fusion.11
  164.6 1.7 convolution_dynamic-update-slice_fusion.9
  166.3 1.6 convolution_dynamic-update-slice_fusion.8
  169.6 1.6 convolution_dynamic-update-slice_fusion.6
  171.2 1.9 convolution_dynamic-update-slice_fusion.5
  174.7 1.6 convolution_dynamic-update-slice_fusion.3
  176.4 1.6 convolution_dynamic-update-slice_fusion.2
  178.0 1.6 convolution_dynamic-update-slice_fusion.1
  179.6 1.7 convolution_dynamic-update-slice_fusion
  181.4 2.0 fusion.4
  183.5 1.9 convolution_add_fusion.25
  185.4 1.9 convolution_add_fusion.24
  187.3 1.9 convolution_add_fusion.23
  210.1 7.5 %collective-permute-done.2 = bf16[256,384]{1,0:T(8,128)(2,1)S(1)} collective-permute-done((bf16[256,384]{1,0:T(8,128)(2,1)S(1)}, bf16[256,384]{1,0:T(8,128)(2,1)S(1)}, u32[]{:S(2)}, u32[]{:S(2)}) %collective-permute-start.2) | collective-permute-done | bytes 196640 | tf_op jit(solution)/shard_map/ppermute | solution.py:11
  217.7 1.8 fusion.40
  219.6 74.8 %reduce-scatter.2.cloned.1.call-done = f32[1296,384]{1,0:T(8,128)} async-done(((f32[10368,384]{1,0:T(8,128)}), f32[1296,384]{1,0:T(8,128)}) %reduce-scatter.2.cloned.1.call-update) | async-done | bytes 1990672 | tf_op jit(solution)/shard_map/reduce_scatter | solution.py:101
  294.4 133.7 %all-reduce.14.cloned.1.call-done = f32[432,384]{1,0:T(8,128)} async-done(((f32[432,384]{1,0:T(8,128)}), f32[432,384]{1,0:T(8,128)}) %all-reduce.14.cloned.1.call-update) | async-done | bytes 663568 | tf_op jit(solution)/shard_map/psum | solution.py:99
  428.1 86.2 %all-reduce.16.cloned.1.call-done = f32[1296,384]{1,0:T(8,128)} async-done(((f32[1296,384]{1,0:T(8,128)}), f32[1296,384]{1,0:T(8,128)}) %all-reduce.16.cloned.1.call-update) | async-done | bytes 1990672 | tf_op jit(solution)/shard_map/psum | solution.py:100
  514.3 3.0 copy.65
  (125 shorter events, 37.0 us)
Async XLA Ops:
  7.2 11.3 %copy-start = (bf16[432,384]{1,0:T(8,128)(2,1)S(1)}, bf16[432,384]{1,0:T(8,128)(2,1)}, u32[]{:S(2)}) copy-start(bf16[432,384]{1,0:T(8,128)(2,1)} %param.8) | copy-start | bytes 995332
  7.2 58.1 %all-gather.2.cloned.1.call-start = ((), (), s32[]{:S(2)}) async-start(), calls=%async_computation.1 | async-start | bytes 8957952 | tf_op jit(solution)/shard_map/all_gather | solution.py:66
  7.9 286.4 %reduce-scatter.2.cloned.1.call-start = ((), (), s32[]{:S(2)}) async-start(), calls=%async_computation.3 | async-start | bytes 17915904 | tf_op jit(solution)/shard_map/reduce_scatter | solution.py:101
  9.7 6.6 %collective-permute-start = (bf16[256,16]{0,1:T(8,128)(2,1)S(1)}, bf16[256,16]{0,1:T(8,128)(2,1)S(1)}, u32[]{:S(2)}, u32[]{:S(2)}) collective-permute-start(bf16[256,16]{0,1:T(8,128)(2,1)S(1)} %slice.384), channel_id=1, source_target_pairs={{0,1},{1,2},{2,3},{4,5},{5,6},{6,7},{8,9},{9,10},{10,11},{12,13},{... | collective-permute-start | bytes 24584 | tf_op jit(solution)/shard_map/ppermute | solution.py:11
  18.5 2.0 copy-start.13
  20.5 7.4 %collective-permute-start.1 = (bf16[256,384]{1,0:T(8,128)(2,1)S(1)}, bf16[256,384]{1,0:T(8,128)(2,1)S(1)}, u32[]{:S(2)}, u32[]{:S(2)}) collective-permute-start(bf16[256,384]{1,0:T(8,128)(2,1)S(1)} %slice.517), channel_id=1, source_target_pairs={{0,1},{1,2},{2,3},{4,5},{5,6},{6,7},{8,9},{9,10},{10,11},{12,13},{... | collective-permute-start | bytes 589832 | tf_op jit(solution)/shard_map/ppermute | solution.py:11
  30.2 43.8 %copy-start.9 = (bf16[1297,384]{1,0:T(8,128)(2,1)}, bf16[1297,384]{1,0:T(8,128)(2,1)S(1)}, u32[]{:S(2)}) copy-start(bf16[1297,384]{1,0:T(8,128)(2,1)S(1)} %concatenate.47) | copy-start | bytes 2988292
  65.3 8.7 %copy-start.2 = (bf16[10368,384]{1,0:T(8,128)(2,1)S(1)}, bf16[10368,384]{1,0:T(8,128)(2,1)}, u32[]{:S(2)}) copy-start(bf16[10368,384]{1,0:T(8,128)(2,1)} %all-gather.2.cloned.1.call-done) | copy-start | bytes 23887876
  135.3 3.1 copy-start.10
  135.3 3.1 copy-start.11
  181.3 2.1 copy-start.7
  181.3 246.8 %all-reduce.14.cloned.1.call-start = ((), (), s32[]{:S(2)}) async-start(), calls=%async_computation.2 | async-start | bytes 1327104 | tf_op jit(solution)/shard_map/psum | solution.py:99
  183.4 1.9 copy-start.6
  183.4 5.7 %slice-start = ((s8[7962624]{0:T(1024)(128)(4,1)}), s8[4194304]{0:T(1024)(128)(4,1)S(1)}, s32[]{:S(2)}) async-start(s8[7962624]{0:T(1024)(128)(4,1)} %bitcast.44), calls=%async_computation.5 | async-start | bytes 8388608
  185.4 1.9 copy-start.5
  185.4 3.8 slice-start.1
  187.3 1.9 copy-start.4
  189.2 1.3 copy-start.3
  192.8 1.3 copy-start.8
  208.5 9.2 %copy-start.14 = (bf16[1024,432]{0,1:T(8,128)(2,1)S(1)}, bf16[1024,432]{0,1:T(8,128)(2,1)}, u32[]{:S(2)}) copy-start(bf16[1024,432]{0,1:T(8,128)(2,1)} %copy-done.13) | copy-start | bytes 2654212
  208.5 9.2 %copy-start.15 = (f32[1024,384]{1,0:T(8,128)S(1)}, f32[1024,384]{1,0:T(8,128)}, u32[]{:S(2)}) copy-start(f32[1024,384]{1,0:T(8,128)} %get-tuple-element.12) | copy-start | bytes 4718596
  208.5 9.2 %collective-permute-start.2 = (bf16[256,384]{1,0:T(8,128)(2,1)S(1)}, bf16[256,384]{1,0:T(8,128)(2,1)S(1)}, u32[]{:S(2)}, u32[]{:S(2)}) collective-permute-start(bf16[256,384]{1,0:T(8,128)(2,1)S(1)} %slice.1014), channel_id=1, source_target_pairs={{1,0},{2,1},{3,2},{5,4},{6,5},{7,6},{9,8},{10,9},{11,10},{13,12},{... | collective-permute-start | bytes 589832 | tf_op jit(solution)/shard_map/ppermute | solution.py:11
  219.5 294.8 %all-reduce.16.cloned.1.call-start = ((), (), s32[]{:S(2)}) async-start(), calls=%async_computation.4 | async-start | bytes 3981312 | tf_op jit(solution)/shard_map/psum | solution.py:100
  428.1 89.2 %copy-start.12 = (f32[432,384]{1,0:T(8,128)S(1)}, f32[432,384]{1,0:T(8,128)}, u32[]{:S(2)}) copy-start(f32[432,384]{1,0:T(8,128)} %all-reduce.14.cloned.1.call-done) | copy-start | bytes 1990660
  514.3 3.9 copy-start.1
Sparse Core Ops, SparseCore 0:
  9.9 55.3 all-gather.1
  181.4 112.8 reduce-scatter.1
  301.0 127.0 all-reduce.13
  430.4 83.9 all-reduce.15
where the time goes:
time: 528 us; the launch traced here: 525 us
  waiting for transfers between devices  342 us (65%)
  matrix products  145 us (27%)
  between operations  15.4 us (3%)
  starting transfers between devices  10.6 us (2%)
  local copies, waits for them, and re-layouts  10 us (2%)
    psum x1, waiting for transfers between devices, shards(): grad_in = lax.psum(cross_dot(patch_in, dz_first), ('clip', 'tm'))  134 us
    psum x1, waiting for transfers between devices, shards(): summed = lax.psum(local_mid, 'tm')  86.2 us
    reduce_scatter x1, waiting for transfers between devices, shards(): grad_mid = lax.psum_scatter(summed, 'clip', scatter_dimension=0, tiled=True)  74.8 us
    dot_general x27, matrix products, shards(): jnp.dot(act_taps[k], w_full[k * chans:(k + 1) * chans], preferred_element...  70 us
    dot_general x28, matrix products, cross_dot(): lax.dot_general(left, right, (((0,), (0,)), ((), ())), preferred_element_...  47.7 us
    all_gather x1, waiting for transfers between devices, shards(): w_full = lax.all_gather(w_mid, 'clip', axis=0, tiled=True)  35.1 us
    dot_general x27, matrix products, shards(): lax.dot_general(piece, w_full[k * chans:(k + 1) * chans], (((1,), (1,)),...  25.7 us
    ppermute x3, waiting for transfers between devices, passed_along(): return lax.ppermute(block, axis, route)  11 us
  transfers between devices with their start and end apart: 7, of which 6 were waited for; matrix products, arithmetic and copies ran while one was open for 7% of the time, Pallas kernels for 0%

commit v1 on v0

--- a/solution.py
+++ b/solution.py
@@ -97,7 +97,15 @@
     sig = jax.nn.sigmoid(z_first)
     dz_first = (dact * sig * (1.0 + z_first * (1.0 - sig))).astype(jnp.bfloat16)
     grad_in = lax.psum(cross_dot(patch_in, dz_first), ("clip", "tm"))
-    summed = lax.psum(local_mid, "tm")
+
+    def _put_region(state):
+        n_shards = lax.psum(1, "tm")
+        r2 = state
+        for h in [u for u in (1, 2, 4, 8, 16) if u < n_shards]:
+            r2 = r2 + lax.ppermute(r2, "tm", [(d, d ^ h) for d in range(n_shards)])
+        return r2
+
+    summed = _put_region(local_mid)
     grad_mid = lax.psum_scatter(summed, "clip", scatter_dimension=0, tiled=True)
     return (grad_mid, grad_in)
 

time: 528 us -> 1470 us (2.78)
  waiting for transfers between devices: 342 us -> 1270 us
  other arithmetic: 2.07 us -> 30.5 us
  matrix products: 145 us -> 118 us
    ppermute x0 -> x2, waiting for transfers between devices: none -> 994 us  [_put_region(): r2 = r2 + lax.ppermute(r2, 'tm', [(d, d ^ h) for d in range(n_shards)])]
    psum x1 -> x0, waiting for transfers between devices: 86.2 us -> none  [shards(): summed = lax.psum(local_mid, 'tm')]
    reduce_scatter x1, waiting for transfers between devices: 74.8 us -> 119 us  [shards(): grad_mid = lax.psum_scatter(summed, 'clip', scatter_dimension=0, tiled=True)]
    add x0 -> x2, other arithmetic: none -> 28.4 us  [_put_region(): r2 = r2 + lax.ppermute(r2, 'tm', [(d, d ^ h) for d in range(n_shards)])]
    dot_general x28, matrix products: 47.7 us -> 25 us  [cross_dot(): lax.dot_general(left, right, (((0,), (0,)), ((), ())), preferred_element_...]
    psum x1, waiting for transfers between devices: 134 us -> 112 us  [shards(): grad_in = lax.psum(cross_dot(patch_in, dz_first), ('clip', 'tm'))]
  transfers between devices with their start and end apart: 7 -> 8, of which waited for: 6 -> 7; matrix products, arithmetic and copies ran while one was open for 7% -> 3% of each run, Pallas kernels for 0% -> 0%
where the time goes in v1:
time: 1470 us; the launch traced here: 1460 us
  waiting for transfers between devices  1270 us (86%)
  matrix products  118 us (8%)
  other arithmetic  30.5 us (2%)
  between operations  15.5 us (1%)
    ppermute x2, waiting for transfers between devices, _put_region(): r2 = r2 + lax.ppermute(r2, 'tm', [(d, d ^ h) for d in range(n_shards)])  994 us
    reduce_scatter x1, waiting for transfers between devices, shards(): grad_mid = lax.psum_scatter(summed, 'clip', scatter_dimension=0, tiled=True)  119 us
    psum x1, waiting for transfers between devices, shards(): grad_in = lax.psum(cross_dot(patch_in, dz_first), ('clip', 'tm'))  112 us
    dot_general x27, matrix products, shards(): jnp.dot(act_taps[k], w_full[k * chans:(k + 1) * chans], preferred_element...  69.9 us
    all_gather x1, waiting for transfers between devices, shards(): w_full = lax.all_gather(w_mid, 'clip', axis=0, tiled=True)  35.1 us
  transfers between devices with their start and end apart: 8, of which 7 were waited for; matrix products, arithmetic and copies ran while one was open for 3% of the time, Pallas kernels for 0%

profile of v1, /device:TPU:0, one launch (start us, length us, event | category | flops | bytes accessed | tf_op | source)
XLA Modules:
  0.0 1463.5 jit_solution(13236428776917786143)
XLA Ops:
  8.6 0.9 constant_dynamic-slice_fusion
  9.7 4.9 collective-permute-start
  14.7 1.1 constant_dynamic-slice_fusion.1
  18.5 2.0 multiply_convert_fusion
  20.5 3.9 collective-permute-start.1
  24.4 3.4 collective-permute-done.1
  27.8 2.3 concatenate.47
  30.2 35.1 %all-gather.2.cloned.1.call-done = bf16[10368,384]{1,0:T(8,128)(2,1)} async-done(((bf16[1296,384]{1,0:T(8,128)(2,1)}), bf16[10368,384]{1,0:T(8,128)(2,1)}) %all-gather.2.cloned.1.call-update) | async-done | bytes 7962640 | tf_op jit(solution)/shard_map/all_gather | solution.py:66
  65.3 3.0 fusion.52
  68.2 2.8 fusion.51
  71.1 2.8 fusion.50
  73.9 1.9 fusion.49
  75.8 1.9 fusion.132
  77.6 1.9 fusion.129
  79.5 1.9 fusion.126
  81.4 1.8 fusion.123
  83.3 1.9 fusion.120
  85.2 1.9 fusion.117
  87.1 1.9 fusion.114
  89.0 1.9 fusion.111
  90.8 1.9 fusion.108
  92.7 1.9 fusion.105
  94.6 1.9 fusion.102
  96.5 1.9 fusion.99
  98.4 1.9 fusion.96
  100.3 2.1 fusion.93
  102.4 1.8 fusion.90
  104.3 1.9 fusion.87
  106.2 1.9 fusion.84
  108.0 1.9 fusion.46
  109.9 1.9 fusion.47
  111.8 1.9 fusion.48
  113.7 1.9 fusion.45
  115.5 1.9 fusion.43
  117.4 17.9 %broadcast_multiply_fusion = (bf16[1024,384]{1,0:T(8,128)(2,1)S(1)}, bf16[1024,384]{1,0:T(8,128)(2,1)S(1)}, bf16[1024,384]{1,0:T(8,128)(2,1)S(1)}, bf16[1024,384...) fusion(bf16[1024]{0:T(1024)(128)(2,1)S(1)} %get-tuple-element.1, ...), kind=kOutput, calls=%fused_computation.165 | convolution fusion | flops 319684608 | bytes 50843648 | tf_op jit(solution)/shard_map/dot_general | solution.py:69
  135.3 2.3 convolution_dynamic-update-slice_fusion.26
  137.6 0.8 convolution_dynamic-update-slice_fusion.25
  140.8 0.8 convolution_dynamic-update-slice_fusion.21
  141.6 0.8 convolution_dynamic-update-slice_fusion.20
  143.2 0.8 convolution_dynamic-update-slice_fusion.18
  144.0 0.8 convolution_dynamic-update-slice_fusion.17
  145.7 0.8 convolution_dynamic-update-slice_fusion.15
  146.5 0.8 convolution_dynamic-update-slice_fusion.14
  148.1 0.8 convolution_dynamic-update-slice_fusion.12
  148.9 0.8 convolution_dynamic-update-slice_fusion.11
  150.5 0.8 convolution_dynamic-update-slice_fusion.9
  151.3 0.8 convolution_dynamic-update-slice_fusion.8
  153.0 0.8 convolution_dynamic-update-slice_fusion.6
  153.8 1.0 convolution_dynamic-update-slice_fusion.5
  158.0 0.8 convolution_dynamic-update-slice_fusion
  158.8 5.8 copy-done.2
  164.6 1.5 collective-permute-start.2
  166.0 342.6 %collective-permute-done.2 = f32[10368,384]{1,0:T(8,128)S(1)} collective-permute-done((f32[10368,384]{1,0:T(8,128)S(1)}, f32[10368,384]{1,0:T(8,128)S(1)}, u32[]{:S(2)}, u32[]{:S(2)}) %collective-permute-start.2) | collective-permute-done | bytes 15925280 | tf_op jit(solution)/shard_map/ppermute | solution.py:105
  508.7 11.3 add.685
  520.0 2.4 collective-permute-start.3
  536.3 1.0 convolution_add_fusion.10
  545.3 1.4 collective-permute-start.4
  546.8 6.5 collective-permute-done.4
  553.4 1.8 fusion.40
  555.2 651.7 %collective-permute-done.3 = f32[10368,384]{1,0:T(8,128)} collective-permute-done((f32[10368,384]{1,0:T(8,128)}, f32[10368,384]{1,0:T(8,128)}, u32[]{:S(2)}, u32[]{:S(2)}) %collective-permute-start.3) | collective-permute-done | bytes 15925280 | tf_op jit(solution)/shard_map/ppermute | solution.py:105
  1206.9 17.2 %add.686 = f32[10368,384]{1,0:T(8,128)} add(f32[10368,384]{1,0:T(8,128)} %add.685, f32[10368,384]{1,0:T(8,128)} %collective-permute-done.3) | non-fusion elementwise | flops 3981312 | bytes 47775744 | tf_op jit(solution)/shard_map/add | solution.py:105
  1224.1 112.2 %all-reduce.13.cloned.1.call-done = f32[432,384]{1,0:T(8,128)} async-done(((f32[432,384]{1,0:T(8,128)}), f32[432,384]{1,0:T(8,128)}) %all-reduce.13.cloned.1.call-update) | async-done | bytes 663568 | tf_op jit(solution)/shard_map/psum | solution.py:99
  1336.2 118.6 %reduce-scatter.2.cloned.1.call-done = f32[1296,384]{1,0:T(8,128)} async-done(((f32[10368,384]{1,0:T(8,128)}), f32[1296,384]{1,0:T(8,128)}) %reduce-scatter.2.cloned.1.call-update) | async-done | bytes 1990672 | tf_op jit(solution)/shard_map/reduce_scatter | solution.py:109
  1454.8 2.0 copy.64
  (127 shorter events, 34.9 us)
Async XLA Ops:
  7.2 11.3 copy-start
  7.2 58.1 %all-gather.2.cloned.1.call-start = ((), (), s32[]{:S(2)}) async-start(), calls=%async_computation.1 | async-start | bytes 8957952 | tf_op jit(solution)/shard_map/all_gather | solution.py:66
  7.9 1328.3 %all-reduce.13.cloned.1.call-start = ((), (), s32[]{:S(2)}) async-start(), calls=%async_computation.3 | async-start | bytes 1327104 | tf_op jit(solution)/shard_map/psum | solution.py:99
  9.7 6.6 collective-permute-start
  18.5 2.0 copy-start.13
  20.5 7.3 collective-permute-start.1
  30.2 45.6 %copy-start.10 = (bf16[1297,384]{1,0:T(8,128)(2,1)}, bf16[1297,384]{1,0:T(8,128)(2,1)S(1)}, u32[]{:S(2)}) copy-start(bf16[1297,384]{1,0:T(8,128)(2,1)S(1)} %concatenate.47) | copy-start | bytes 2988292
  65.3 8.6 copy-start.3
  135.3 2.3 copy-start.11
  135.3 2.3 copy-start.12
  158.0 364.4 %slice-start = ((s8[7962624]{0:T(1024)(128)(4,1)}), s8[4194304]{0:T(1024)(128)(4,1)S(1)}, s32[]{:S(2)}) async-start(s8[7962624]{0:T(1024)(128)(4,1)} %bitcast.44), calls=%async_computation.4 | async-start | bytes 8388608
  158.8 5.8 copy-start.2
  164.6 357.8 %slice-start.1 = ((s8[7962624]{0:T(1024)(128)(4,1)}), s8[3768320]{0:T(1024)(128)(4,1)S(1)}, s32[]{:S(2)}) async-start(s8[7962624]{0:T(1024)(128)(4,1)} %bitcast.44), calls=%async_computation.5 | async-start | bytes 7536640
  164.6 357.8 %copy-start.9 = (bf16[1024,384]{1,0:T(8,128)(2,1)S(1)}, bf16[1024,384]{1,0:T(8,128)(2,1)}, u32[]{:S(2)}) copy-start(bf16[1024,384]{1,0:T(8,128)(2,1)} %get-tuple-element.10) | copy-start | bytes 2359300
  164.6 344.1 %collective-permute-start.2 = (f32[10368,384]{1,0:T(8,128)S(1)}, f32[10368,384]{1,0:T(8,128)S(1)}, u32[]{:S(2)}, u32[]{:S(2)}) collective-permute-start(f32[10368,384]{1,0:T(8,128)S(1)} %convolution_dynamic-update-slice_fusion), channel_id=1, source_target_pairs={{0,1},{1,0},{2,3},{3,2},{4,5},{5,4},{6,7},{7,6},{8,9},{9,8},{10,11... | collective-permute-start | bytes 47775752 | tf_op jit(solution)/shard_map/ppermute | solution.py:105
  520.0 3.2 copy-start.8
  520.0 686.9 %collective-permute-start.3 = (f32[10368,384]{1,0:T(8,128)}, f32[10368,384]{1,0:T(8,128)}, u32[]{:S(2)}, u32[]{:S(2)}) collective-permute-start(f32[10368,384]{1,0:T(8,128)} %add.685), channel_id=1, source_target_pairs={{0,2},{1,3},{2,0},{3,1},{4,6},{5,7},{6,4},{7,5},{8,10},{9,11},{10,... | collective-permute-start | bytes 47775752 | tf_op jit(solution)/shard_map/ppermute | solution.py:105
  523.2 1.1 copy-start.7
  524.3 1.1 copy-start.6
  525.4 1.1 copy-start.5
  526.6 1.1 copy-start.4
  545.3 8.1 copy-start.14
  545.3 8.1 copy-start.15
  545.3 8.0 collective-permute-start.4
  555.1 899.7 %reduce-scatter.2.cloned.1.call-start = ((), (), s32[]{:S(2)}) async-start(), calls=%async_computation.2 | async-start | bytes 17915904 | tf_op jit(solution)/shard_map/reduce_scatter | solution.py:109
  1224.1 232.7 %copy-start.1 = (bf16[432,384]{1,0:T(8,128)(2,1)S(1)}, bf16[432,384]{1,0:T(8,128)(2,1)}, u32[]{:S(2)}) copy-start(bf16[432,384]{1,0:T(8,128)(2,1)} %param.8) | copy-start | bytes 995332
Sparse Core Ops, SparseCore 0:
  9.9 55.3 all-gather.1
  555.3 780.9 all-reduce.12
  1340.9 113.8 reduce-scatter.1
